TPU v7x, 32 devices: a whole 2x2x4 slice. The times are simulated.
32 devices in a mesh: space: 8 (over z, x), orb: 4 (over y, core).
Axes of the slice: x: 2, y: 2, z: 4, core: 2. Of those that a mesh axis runs over, the one named last changes fastest.
Arguments:
- psi: bfloat16 [16, 48, 48, 512], P('space', None, None, 'orb'), may hold values from -6 to 6
- potential: float32 [16, 48, 48], P('space'), may hold values from 0 to 2
- beta: bfloat16 [8, 16, 48, 48], P(None, 'space'), may hold values from -0.21875 to 0.21875
- strength: float32 [8], replicated, may hold values from 0.5 to 4
- atom_slab: int32 [8], replicated, may hold values from 0 to 7, each once
- pattern: int32 [12, 2], replicated, may hold values from 0 to 3, as said below
- q_tiles: bfloat16 [12, 128, 128], replicated, may hold values from -0.3125 to 0.3125
Outputs:
- rotated: bfloat16 [16, 48, 48, 512], P('space', None, None, 'orb')
Inputs may be any that keep to these rules, and one draw needn't show every extreme that they name: `pattern`: the 12 tile coordinates are distinct, each in 0 to 3, and every diagonal tile is among them.
All inputs are finite; a program needn't handle non-finite values.
Results may differ from a plain program's by a relative error of at most 0.0064.
Values may be sent and summed in bfloat16 or wider, within the bound.
No kernel may reach another device: no remote copies, remote signals or barrier semaphores. Data moves between devices by JAX's collectives and lax.ppermute only.
A program may use at most 64 MiB of HBM per device.

v0:
```python
import jax
import jax.numpy as jnp
from jax import lax
from jax.sharding import PartitionSpec as P


def passed_along(array, axis, by):
    length = lax.axis_size(axis)
    pairs = [(i, i + by) for i in range(length) if 0 <= i + by < length]
    return lax.ppermute(array, axis, pairs)


def with_halo(block, sides, width):
    for axis, dim in sides:
        count = lax.axis_size(axis)
        forward = [(i, i + 1) for i in range(count - 1)]
        backward = [(target, source) for source, target in forward]
        low = lax.ppermute(
            lax.slice_in_dim(block, block.shape[dim] - width, None, axis=dim), axis, forward
        )
        high = lax.ppermute(lax.slice_in_dim(block, 0, width, axis=dim), axis, backward)
        block = jnp.concatenate([low, block, high], axis=dim)
    return block


def gather_partials(partial_proj):
    proj = partial_proj
    proj = proj + passed_along(partial_proj, "space", 1)
    proj = proj + passed_along(partial_proj, "space", -1)
    proj = proj + passed_along(partial_proj, "space", 2)
    proj = proj + passed_along(partial_proj, "space", -2)
    return proj


def apply_filter(v2, planes, potential_flat, beta_m, strength):
    f = planes.astype(jnp.float32)
    padded = with_halo(planes, (("space", 0),), 1).astype(jnp.float32)
    pxy = jnp.pad(f, ((0, 0), (1, 1), (1, 1), (0, 0)))
    beside = padded[2:] + padded[:-2]
    beside = beside + pxy[:, 2:, 1:-1] + pxy[:, :-2, 1:-1] + pxy[:, 1:-1, 2:] + pxy[:, 1:-1, :-2]
    kinetic = -0.5 * (beside - 6.0 * f)
    partial_proj = jnp.dot(beta_m, v2, preferred_element_type=jnp.float32)
    proj = gather_partials(partial_proj)
    coef = (strength[:, None] * proj).astype(jnp.bfloat16)
    nonlocal_term = lax.dot_general(
        beta_m, coef, (((0,), (0,)), ((), ())), preferred_element_type=jnp.float32
    )
    total = (
        kinetic.reshape(v2.shape) + potential_flat[:, None] * f.reshape(v2.shape) + nonlocal_term
    )
    return ((total - 4.0 * f.reshape(v2.shape)) / 4.0).astype(jnp.bfloat16)


def shards(psi, potential, beta, strength, atom_slab, pattern, q_tiles):
    planes_z, width_x, width_y, orb_cols = psi.shape
    cells = planes_z * width_x * width_y
    my_slab = lax.axis_index("space")
    active = jnp.abs(my_slab - atom_slab) <= 1
    flat_beta = beta.reshape(beta.shape[0], cells)
    beta_m = jnp.where(active[:, None], flat_beta, jnp.zeros_like(flat_beta))
    potential_flat = potential.reshape(cells)
    first = apply_filter(psi.reshape(cells, orb_cols), psi, potential_flat, beta_m, strength)
    second = apply_filter(
        first, first.reshape(planes_z, width_x, width_y, orb_cols), potential_flat, beta_m, strength
    )
    tile = q_tiles.shape[1]
    blocks = orb_cols * lax.axis_size("orb") // tile
    my_col = lax.axis_index("orb")
    ids = jnp.arange(blocks, dtype=jnp.int32)
    rows_hot = (pattern[:, 0][:, None] == ids[None, :]).astype(jnp.float32)
    mine = (pattern[:, 1] == my_col).astype(jnp.float32)
    column_q = jnp.einsum("ki,k,kab->iab", rows_hot, mine, q_tiles.astype(jnp.float32))
    column_q = column_q.reshape(blocks * tile, tile).astype(jnp.bfloat16)
    result = jnp.dot(
        lax.all_gather(second, "orb", axis=1, tiled=True),
        column_q,
        preferred_element_type=jnp.float32,
    )
    return result.astype(jnp.bfloat16).reshape(planes_z, width_x, width_y, orb_cols)


def solution(mesh):
    placed = (
        P("space", None, None, "orb"),
        P("space", None, None),
        P(None, "space", None, None),
        P(),
        P(),
        P(),
        P(),
    )
    return jax.shard_map(
        shards, mesh=mesh, in_specs=placed, out_specs=P("space", None, None, "orb"), check_vma=False
    )
```

profile of v0, /device:TPU:0, one launch (start us, length us, event | category | flops | bytes accessed | tf_op | source)
XLA Modules:
  0.0 137.3 jit_solution(8860781879933464515)
XLA Ops:
  6.5 2.5 %fusion.30 = (bf16[1,48,48,128]{3,2,1,0:T(8,128)(2,1)}, bf16[1,48,48,128]{3,2,1,0:T(8,128)(2,1)}) fusion(bf16[2,48,48,128]{3,2,1,0:T(8,128)(2,1)} %param.7), kind=kLoop, calls=%fused_computation.59 | loop fusion | bytes 2359296 | tf_op jit(solution)/shard_map/slice | solution.py:19
  9.0 5.7 %collective-permute-start = (bf16[1,48,48,128]{3,2,1,0:T(8,128)(2,1)}, bf16[1,48,48,128]{3,2,1,0:T(8,128)(2,1)}, u32[]{:S(2)}, u32[]{:S(2)}) collective-permute-start(bf16[1,48,48,128]{3,2,1,0:T(8,128)(2,1)} %get-tuple-element.9), channel_id=1, source_target_pairs={{0,4},{4,8},{8,12},{12,16},{16,20},{20,24},{24,28},{1,5},{5,9},{9,... | collective-permute-start | bytes 1769480 | tf_op jit(solution)/shard_map/ppermute | solution.py:18
  14.7 1.3 collective-permute-start.1
  16.7 4.5 %collective-permute-start.2 = (f32[8,128]{1,0:T(8,128)S(1)}, f32[8,128]{1,0:T(8,128)S(1)}, u32[]{:S(2)}, u32[]{:S(2)}) collective-permute-start(f32[8,128]{1,0:T(8,128)S(1)} %convolution_bitcast_fusion), channel_id=1, source_target_pairs={{0,4},{4,8},{8,12},{12,16},{16,20},{20,24},{24,28},{1,5},{5,9},{9,... | collective-permute-start | bytes 12296 | tf_op jit(solution)/shard_map/ppermute | solution.py:10
  21.2 1.3 collective-permute-start.3
  22.5 6.2 %collective-permute-start.4 = (f32[8,128]{1,0:T(8,128)S(1)}, f32[8,128]{1,0:T(8,128)}, u32[]{:S(2)}, u32[]{:S(2)}) collective-permute-start(f32[8,128]{1,0:T(8,128)S(1)} %convolution_bitcast_fusion), channel_id=1, source_target_pairs={{0,8},{4,12},{8,16},{12,20},{16,24},{20,28},{1,9},{5,13},{9,17},{1... | collective-permute-start | bytes 12296 | tf_op jit(solution)/shard_map/ppermute | solution.py:10
  28.9 1.8 %reshape.42 = bf16[8,4608]{1,0:T(8,128)(2,1)} reshape(bf16[8,2,48,48]{3,2,1,0:T(8,128)(2,1)} %param.9) | data formatting | bytes 147456 | tf_op jit(solution)/shard_map/reshape | solution.py:59
  30.7 1.5 %mul.50 = f32[4608]{0:T(1024)} reshape(f32[2,48,48]{2,1,0:T(8,128)} %param.8) | data formatting | bytes 36864 | tf_op jit(solution)/shard_map/mul | solution.py:49
  32.2 7.3 %collective-permute-done = bf16[1,48,48,128]{3,2,1,0:T(8,128)(2,1)} collective-permute-done((bf16[1,48,48,128]{3,2,1,0:T(8,128)(2,1)}, bf16[1,48,48,128]{3,2,1,0:T(8,128)(2,1)}, u32[]{:S(2)}, u32[]{:S(2)}) %collective-permute-start) | collective-permute-done | bytes 589856 | tf_op jit(solution)/shard_map/ppermute | solution.py:18
  39.5 1.3 collective-permute-start.5
  40.8 1.6 %maximum_convert_fusion = f32[4,48,48,128]{3,2,1,0:T(8,128)S(1)} fusion(bf16[1,48,48,128]{3,2,1,0:T(8,128)(2,1)} %collective-permute-done.1, bf16[2,48,48,128]{3,2,1,0:T(8,128)(2,1)S(1)} %copy-done, bf16[1,48,48,128]{3,2,1,0:T(8,128)(2,1)} %collective-permute-done), kind=kLoop, calls=%fused_computation.34 | loop fusion | flops 3538944 | bytes 7077888 | tf_op jit(solution)/shard_map/convert_element_type | solution.py:37
  43.5 2.0 %fusion.19 = (f32[4608,128]{1,0:T(8,128)S(1)}, f32[4608,128]{1,0:T(8,128)S(1)}) fusion(f32[2,48,48,128]{3,2,1,0:T(8,128)S(1)} %fusion.12, f32[4608]{0:T(1024)S(1)} %copy-done.4, bf16[2,48,48,128]{3,2,1,0:T(8,128)(2,1)S(1)} %copy-done), kind=kLoop, calls=%fused_computation.38 | loop fusion | flops 2359296 | bytes 8275968 | tf_op jit(solution)/shard_map/add | solution.py:49
  45.6 1.4 %fusion.4 = bf16[4608,128]{1,0:T(8,128)(2,1)S(1)} fusion(f32[4608,128]{1,0:T(8,128)S(1)} %get-tuple-element.8, f32[4608,128]{1,0:T(8,128)S(1)} %get-tuple-element.7, f32[8,128]{1,0:T(8,128)S(1)} %collective-permute-done.5, f32[8,128]{1,0:T(8,128)} %collective-permute-done.4, f32[8,128]{1,0:T(8,128)S(1)} %collective-permute-done.3, ...), kind=kOutput, calls=%fused_computation.6 | convolution fusion | flops 11839488 | bytes 5992488 | tf_op jit(solution)/shard_map/dot_general | solution.py:45
  47.1 4.4 %collective-permute-start.6 = (bf16[1,48,48,128]{3,2,1,0:T(8,128)(2,1)S(1)}, bf16[1,48,48,128]{3,2,1,0:T(8,128)(2,1)S(1)}, u32[]{:S(2)}, u32[]{:S(2)}) collective-permute-start(bf16[1,48,48,128]{3,2,1,0:T(8,128)(2,1)S(1)} %bitcast.34), channel_id=1, source_target_pairs={{0,4},{4,8},{8,12},{12,16},{16,20},{20,24},{24,28},{1,5},{5,9},{9,... | collective-permute-start | bytes 1769480 | tf_op jit(solution)/shard_map/ppermute | solution.py:18
  51.5 1.3 collective-permute-start.7
  53.2 5.6 %collective-permute-start.10 = (f32[8,128]{1,0:T(8,128)S(1)}, f32[8,128]{1,0:T(8,128)S(1)}, u32[]{:S(2)}, u32[]{:S(2)}) collective-permute-start(f32[8,128]{1,0:T(8,128)S(1)} %fusion.28), channel_id=1, source_target_pairs={{0,8},{4,12},{8,16},{12,20},{16,24},{20,28},{1,9},{5,13},{9,17},{1... | collective-permute-start | bytes 12296 | tf_op jit(solution)/shard_map/ppermute | solution.py:10
  58.7 1.3 collective-permute-start.11
  60.0 3.5 %collective-permute-start.8 = (f32[8,128]{1,0:T(8,128)S(1)}, f32[8,128]{1,0:T(8,128)S(1)}, u32[]{:S(2)}, u32[]{:S(2)}) collective-permute-start(f32[8,128]{1,0:T(8,128)S(1)} %fusion.28), channel_id=1, source_target_pairs={{0,4},{4,8},{8,12},{12,16},{16,20},{20,24},{24,28},{1,5},{5,9},{9,... | collective-permute-start | bytes 12296 | tf_op jit(solution)/shard_map/ppermute | solution.py:10
  63.7 12.1 %collective-permute-done.6 = bf16[1,48,48,128]{3,2,1,0:T(8,128)(2,1)S(1)} collective-permute-done((bf16[1,48,48,128]{3,2,1,0:T(8,128)(2,1)S(1)}, bf16[1,48,48,128]{3,2,1,0:T(8,128)(2,1)S(1)}, u32[]{:S(2)}, u32[]{:S(2)}) %collective-permute-start.6) | collective-permute-done | bytes 589856 | tf_op jit(solution)/shard_map/ppermute | solution.py:18
  75.8 1.3 collective-permute-start.9
  78.5 3.3 %collective-permute-done.9 = f32[8,128]{1,0:T(8,128)S(1)} collective-permute-done((f32[8,128]{1,0:T(8,128)S(1)}, f32[8,128]{1,0:T(8,128)S(1)}, u32[]{:S(2)}, u32[]{:S(2)}) %collective-permute-start.9) | collective-permute-done | bytes 4128 | tf_op jit(solution)/shard_map/ppermute | solution.py:10
  81.8 3.2 %fusion.5 = bf16[4608,128]{1,0:T(8,128)(2,1)} fusion(f32[4608,128]{1,0:T(8,128)S(1)} %bitcast.32, bf16[4608,128]{1,0:T(8,128)(2,1)S(1)} %fusion.4, f32[4608]{0:T(1024)S(1)} %copy-done.4, f32[8,128]{1,0:T(8,128)S(1)} %collective-permute-done.11, f32[8,128]{1,0:T(8,128)S(1)} %collective-permute-done.10, f32[8,128]{1,0:T(8,128)S(1)} %collective-permute-done.9, ...), kind=kOutput, calls=%fused_computation.7 | convolution fusion | flops 14198784 | bytes 4831272 | tf_op jit(solution)/shard_map/dot_general | solution.py:45
  85.6 40.1 %all-gather.2.cloned.1.call-done = bf16[4608,512]{1,0:T(8,128)(2,1)} async-done(((bf16[4608,128]{1,0:T(8,128)(2,1)}), bf16[4608,512]{1,0:T(8,128)(2,1)}) %all-gather.2.cloned.1.call-update) | async-done | bytes 4718608 | tf_op jit(solution)/shard_map/all_gather | solution.py:75
  125.7 4.7 %convolution_convert_fusion = bf16[4608,128]{1,0:T(8,128)(2,1)} fusion(bf16[4608,512]{1,0:T(8,128)(2,1)} %all-gather.2.cloned.1.call-done, bf16[512,128]{1,0:T(8,128)(2,1)S(1)} %bitcast.35), kind=kOutput, calls=%fused_computation.8 | convolution fusion | flops 604569600 | bytes 6029312 | tf_op jit(solution)/shard_map/dot_general | solution.py:74
  (42 shorter events, 4.3 us)
Async XLA Ops:
  6.5 9.5 %copy-start = (bf16[2,48,48,128]{3,2,1,0:T(8,128)(2,1)S(1)}, bf16[2,48,48,128]{3,2,1,0:T(8,128)(2,1)}, u32[]{:S(2)}) copy-start(bf16[2,48,48,128]{3,2,1,0:T(8,128)(2,1)} %param.7) | copy-start | bytes 3538948
  6.5 9.4 %copy-start.7 = (s32[8]{0:T(128)S(1)}, s32[8]{0:T(128)}, u32[]{:S(2)}) copy-start(s32[8]{0:T(128)} %param.11) | copy-start | bytes 100
  6.5 9.4 %copy-start.2 = (bf16[8,2,48,48]{3,2,1,0:T(8,128)(2,1)S(1)}, bf16[8,2,48,48]{3,2,1,0:T(8,128)(2,1)}, u32[]{:S(2)}) copy-start(bf16[8,2,48,48]{3,2,1,0:T(8,128)(2,1)} %param.9) | copy-start | bytes 221188
  6.5 119.2 %all-gather.2.cloned.1.call-start = ((), (), s32[]{:S(2)}) async-start(), calls=%async_computation | async-start | bytes 5898240 | tf_op jit(solution)/shard_map/all_gather | solution.py:75
  9.0 30.5 %collective-permute-start = (bf16[1,48,48,128]{3,2,1,0:T(8,128)(2,1)}, bf16[1,48,48,128]{3,2,1,0:T(8,128)(2,1)}, u32[]{:S(2)}, u32[]{:S(2)}) collective-permute-start(bf16[1,48,48,128]{3,2,1,0:T(8,128)(2,1)} %get-tuple-element.9), channel_id=1, source_target_pairs={{0,4},{4,8},{8,12},{12,16},{16,20},{20,24},{24,28},{1,5},{5,9},{9,... | collective-permute-start | bytes 1769480 | tf_op jit(solution)/shard_map/ppermute | solution.py:18
  14.7 26.1 %collective-permute-start.1 = (bf16[1,48,48,128]{3,2,1,0:T(8,128)(2,1)}, bf16[1,48,48,128]{3,2,1,0:T(8,128)(2,1)}, u32[]{:S(2)}, u32[]{:S(2)}) collective-permute-start(bf16[1,48,48,128]{3,2,1,0:T(8,128)(2,1)} %get-tuple-element.10), channel_id=1, source_target_pairs={{4,0},{8,4},{12,8},{16,12},{20,16},{24,20},{28,24},{5,1},{9,5},{13... | collective-permute-start | bytes 1769480 | tf_op jit(solution)/shard_map/ppermute | solution.py:21
  16.7 28.9 %collective-permute-start.2 = (f32[8,128]{1,0:T(8,128)S(1)}, f32[8,128]{1,0:T(8,128)S(1)}, u32[]{:S(2)}, u32[]{:S(2)}) collective-permute-start(f32[8,128]{1,0:T(8,128)S(1)} %convolution_bitcast_fusion), channel_id=1, source_target_pairs={{0,4},{4,8},{8,12},{12,16},{16,20},{20,24},{24,28},{1,5},{5,9},{9,... | collective-permute-start | bytes 12296 | tf_op jit(solution)/shard_map/ppermute | solution.py:10
  21.2 24.3 %collective-permute-start.3 = (f32[8,128]{1,0:T(8,128)S(1)}, f32[8,128]{1,0:T(8,128)S(1)}, u32[]{:S(2)}, u32[]{:S(2)}) collective-permute-start(f32[8,128]{1,0:T(8,128)S(1)} %convolution_bitcast_fusion), channel_id=1, source_target_pairs={{4,0},{8,4},{12,8},{16,12},{20,16},{24,20},{28,24},{5,1},{9,5},{13... | collective-permute-start | bytes 12296 | tf_op jit(solution)/shard_map/ppermute | solution.py:10
  22.5 23.1 %collective-permute-start.4 = (f32[8,128]{1,0:T(8,128)S(1)}, f32[8,128]{1,0:T(8,128)}, u32[]{:S(2)}, u32[]{:S(2)}) collective-permute-start(f32[8,128]{1,0:T(8,128)S(1)} %convolution_bitcast_fusion), channel_id=1, source_target_pairs={{0,8},{4,12},{8,16},{12,20},{16,24},{20,28},{1,9},{5,13},{9,17},{1... | collective-permute-start | bytes 12296 | tf_op jit(solution)/shard_map/ppermute | solution.py:10
  39.5 6.1 %collective-permute-start.5 = (f32[8,128]{1,0:T(8,128)S(1)}, f32[8,128]{1,0:T(8,128)S(1)}, u32[]{:S(2)}, u32[]{:S(2)}) collective-permute-start(f32[8,128]{1,0:T(8,128)S(1)} %convolution_bitcast_fusion), channel_id=1, source_target_pairs={{8,0},{12,4},{16,8},{20,12},{24,16},{28,20},{9,1},{13,5},{17,9},{2... | collective-permute-start | bytes 12296 | tf_op jit(solution)/shard_map/ppermute | solution.py:10
  42.4 1.1 copy-start.4
  43.5 2.1 %copy-start.1 = (bf16[8,4608]{1,0:T(8,128)(2,1)S(1)}, bf16[8,4608]{1,0:T(8,128)(2,1)}, u32[]{:S(2)}) copy-start(bf16[8,4608]{1,0:T(8,128)(2,1)} %reshape.42) | copy-start | bytes 221188
  43.5 2.1 %copy-start.5 = (f32[8]{0:T(128)S(1)}, f32[8]{0:T(128)}, u32[]{:S(2)}) copy-start(f32[8]{0:T(128)} %param.10) | copy-start | bytes 100
  47.1 28.7 %collective-permute-start.6 = (bf16[1,48,48,128]{3,2,1,0:T(8,128)(2,1)S(1)}, bf16[1,48,48,128]{3,2,1,0:T(8,128)(2,1)S(1)}, u32[]{:S(2)}, u32[]{:S(2)}) collective-permute-start(bf16[1,48,48,128]{3,2,1,0:T(8,128)(2,1)S(1)} %bitcast.34), channel_id=1, source_target_pairs={{0,4},{4,8},{8,12},{12,16},{16,20},{20,24},{24,28},{1,5},{5,9},{9,... | collective-permute-start | bytes 1769480 | tf_op jit(solution)/shard_map/ppermute | solution.py:18
  51.5 25.6 %collective-permute-start.7 = (bf16[1,48,48,128]{3,2,1,0:T(8,128)(2,1)S(1)}, bf16[1,48,48,128]{3,2,1,0:T(8,128)(2,1)S(1)}, u32[]{:S(2)}, u32[]{:S(2)}) collective-permute-start(bf16[1,48,48,128]{3,2,1,0:T(8,128)(2,1)S(1)} %bitcast.33), channel_id=1, source_target_pairs={{4,0},{8,4},{12,8},{16,12},{20,16},{24,20},{28,24},{5,1},{9,5},{13... | collective-permute-start | bytes 1769480 | tf_op jit(solution)/shard_map/ppermute | solution.py:21
  53.2 25.3 %collective-permute-start.10 = (f32[8,128]{1,0:T(8,128)S(1)}, f32[8,128]{1,0:T(8,128)S(1)}, u32[]{:S(2)}, u32[]{:S(2)}) collective-permute-start(f32[8,128]{1,0:T(8,128)S(1)} %fusion.28), channel_id=1, source_target_pairs={{0,8},{4,12},{8,16},{12,20},{16,24},{20,28},{1,9},{5,13},{9,17},{1... | collective-permute-start | bytes 12296 | tf_op jit(solution)/shard_map/ppermute | solution.py:10
  58.7 19.7 %collective-permute-start.11 = (f32[8,128]{1,0:T(8,128)S(1)}, f32[8,128]{1,0:T(8,128)S(1)}, u32[]{:S(2)}, u32[]{:S(2)}) collective-permute-start(f32[8,128]{1,0:T(8,128)S(1)} %fusion.28), channel_id=1, source_target_pairs={{8,0},{12,4},{16,8},{20,12},{24,16},{28,20},{9,1},{13,5},{17,9},{2... | collective-permute-start | bytes 12296 | tf_op jit(solution)/shard_map/ppermute | solution.py:10
  60.0 18.4 %collective-permute-start.8 = (f32[8,128]{1,0:T(8,128)S(1)}, f32[8,128]{1,0:T(8,128)S(1)}, u32[]{:S(2)}, u32[]{:S(2)}) collective-permute-start(f32[8,128]{1,0:T(8,128)S(1)} %fusion.28), channel_id=1, source_target_pairs={{0,4},{4,8},{8,12},{12,16},{16,20},{20,24},{24,28},{1,5},{5,9},{9,... | collective-permute-start | bytes 12296 | tf_op jit(solution)/shard_map/ppermute | solution.py:10
  75.8 6.0 %collective-permute-start.9 = (f32[8,128]{1,0:T(8,128)S(1)}, f32[8,128]{1,0:T(8,128)S(1)}, u32[]{:S(2)}, u32[]{:S(2)}) collective-permute-start(f32[8,128]{1,0:T(8,128)S(1)} %fusion.28), channel_id=1, source_target_pairs={{4,0},{8,4},{12,8},{16,12},{20,16},{24,20},{28,24},{5,1},{9,5},{13... | collective-permute-start | bytes 12296 | tf_op jit(solution)/shard_map/ppermute | solution.py:10
  81.8 3.3 %copy-start.6 = (s32[12,2]{0,1:T(2,128)S(1)}, s32[12,2]{0,1:T(2,128)}, u32[]{:S(2)}) copy-start(s32[12,2]{0,1:T(2,128)} %param.12) | copy-start | bytes 292
  81.8 3.3 %copy-start.3 = (bf16[12,128,128]{2,1,0:T(8,128)(2,1)S(1)}, bf16[12,128,128]{2,1,0:T(8,128)(2,1)}, u32[]{:S(2)}) copy-start(bf16[12,128,128]{2,1,0:T(8,128)(2,1)} %param.13) | copy-start | bytes 1179652
Sparse Core Ops, SparseCore 0:
  85.2 40.5 all-gather.1
where the time goes:
time: 138 us; the launch traced here: 137 us
  waiting for transfers between devices  62.9 us (46%)
  starting transfers between devices  37.6 us (27%)
  between operations  13.7 us (10%)
  matrix products  10.6 us (8%)
  other arithmetic  6.56 us (5%)
  local copies, waits for them, and re-layouts  5.88 us (4%)
    all_gather x1, waiting for transfers between devices, shards(): lax.all_gather(second, 'orb', axis=1, tiled=True)  40.1 us
    ppermute x8, starting transfers between devices, passed_along(): return lax.ppermute(array, axis, pairs)  25 us
    ppermute x2, waiting for transfers between devices, with_halo(): lax.ppermute(lax.slice_in_dim(block, block.shape[dim] - width, None, axis...  19.4 us
    ppermute x2, starting transfers between devices, with_halo(): lax.ppermute(lax.slice_in_dim(block, block.shape[dim] - width, None, axis...  10.1 us
    dot_general x1, matrix products, shards(): jnp.dot(lax.all_gather(second, 'orb', axis=1, tiled=True), column_q, pref...  4.73 us
    dot_general x2, matrix products, apply_filter(): lax.dot_general(beta_m, coef, (((0,), (0,)), ((), ())), preferred_element...  4.63 us
    ppermute x8, waiting for transfers between devices, passed_along(): return lax.ppermute(array, axis, pairs)  3.36 us
  transfers between devices with their start and end apart: 13, of which 4 were waited for; matrix products, arithmetic and copies ran while one was open for 8% of the time, Pallas kernels for 0%

commit v1 on v0

--- a/solution.py
+++ b/solution.py
@@ -1,7 +1,38 @@
+import functools
 import jax
 import jax.numpy as jnp
 from jax import lax
 from jax.sharding import PartitionSpec as P
+
+
+def _cut_ports(vec, dimension_no):
+    carry_out = jax.lax.psum(1, "orb")
+    all_rows = jax.lax.axis_index("orb")
+    local_now, upper, r2 = (carry_out, all_rows, vec.shape[dimension_no])
+    z2 = jnp.zeros(
+        [s * local_now if src_i == dimension_no else s for src_i, s in enumerate(vec.shape)],
+        vec.dtype,
+    )
+    extra = lax.dynamic_update_slice_in_dim(z2, vec, upper * r2, axis=dimension_no)
+    local_next = new = vec
+    for tick in range(1, local_now // 2 + 1):
+        local_next = jax.lax.ppermute(
+            local_next, "orb", [(src_i, (src_i + 1) % local_now) for src_i in range(local_now)]
+        )
+        extra = lax.dynamic_update_slice_in_dim(
+            extra, local_next, (upper - tick) % local_now * r2, axis=dimension_no
+        )
+        if 2 * tick < local_now:
+            new = jax.lax.ppermute(
+                new, "orb", [(src_i, (src_i - 1) % local_now) for src_i in range(local_now)]
+            )
+            extra = lax.dynamic_update_slice_in_dim(
+                extra, new, (upper + tick) % local_now * r2, axis=dimension_no
+            )
+    return extra
+
+
+drive_sites = functools.partial(_cut_ports, dimension_no=1)
 
 
 def passed_along(array, axis, by):
@@ -71,11 +102,7 @@
     mine = (pattern[:, 1] == my_col).astype(jnp.float32)
     column_q = jnp.einsum("ki,k,kab->iab", rows_hot, mine, q_tiles.astype(jnp.float32))
     column_q = column_q.reshape(blocks * tile, tile).astype(jnp.bfloat16)
-    result = jnp.dot(
-        lax.all_gather(second, "orb", axis=1, tiled=True),
-        column_q,
-        preferred_element_type=jnp.float32,
-    )
+    result = jnp.dot(drive_sites(second), column_q, preferred_element_type=jnp.float32)
     return result.astype(jnp.bfloat16).reshape(planes_z, width_x, width_y, orb_cols)
 
 

time: 138 us -> 132 us (0.957)
  between operations: 13.7 us -> 0.34 us
  local copies, waits for them, and re-layouts: 5.88 us -> 13.8 us
  waiting for transfers between devices: 62.9 us -> 58.5 us
  starting transfers between devices: 37.6 us -> 39.6 us
    all_gather x1 -> x0, waiting for transfers between devices: 40.1 us -> none  [shards(): lax.all_gather(second, 'orb', axis=1, tiled=True)]
    ppermute x0 -> x3, waiting for transfers between devices: none -> 35.5 us  [the longest x2 35.5 us: _cut_ports(): jax.lax.ppermute(local_next, 'orb', [(src_i, (src_i + 1) % local_now) for...]
    dynamic_update_slice x0 -> x3, local copies, waits for them, and re-layouts: none -> 3.57 us  [the longest x2 2.37 us: _cut_ports(): lax.dynamic_update_slice_in_dim(extra, local_next, (upper - tick) % local...]
    unnamed x16 -> x22, local copies, waits for them, and re-layouts: 0.03 us -> 2.59 us
    ppermute x0 -> x3, starting transfers between devices: none -> 2.01 us  [the longest x1 1.74 us: _cut_ports(): jax.lax.ppermute(new, 'orb', [(src_i, (src_i - 1) % local_now) for src_i...]
  transfers between devices with their start and end apart: 13 -> 15, of which waited for: 4 -> 5; matrix products, arithmetic and copies ran while one was open for 8% -> 12% of each run, Pallas kernels for 0% -> 0%
where the time goes in v1:
time: 132 us; the launch traced here: 130 us
  waiting for transfers between devices  58.5 us (44%)
  starting transfers between devices  39.6 us (30%)
  local copies, waits for them, and re-layouts  13.8 us (10%)
  matrix products  10.3 us (8%)
  other arithmetic  7.5 us (6%)
    ppermute x2, waiting for transfers between devices, _cut_ports(): jax.lax.ppermute(local_next, 'orb', [(src_i, (src_i + 1) % local_now) for...  35.5 us
    ppermute x8, starting transfers between devices, passed_along(): return lax.ppermute(array, axis, pairs)  25 us
    ppermute x2, waiting for transfers between devices, with_halo(): lax.ppermute(lax.slice_in_dim(block, block.shape[dim] - width, None, axis...  19.7 us
    ppermute x2, starting transfers between devices, with_halo(): lax.ppermute(lax.slice_in_dim(block, block.shape[dim] - width, None, axis...  10.1 us
    dot_general x1, matrix products, shards(): jnp.dot(drive_sites(second), column_q, preferred_element_type=jnp.float32)  4.74 us
    dot_general x2, matrix products, apply_filter(): lax.dot_general(beta_m, coef, (((0,), (0,)), ((), ())), preferred_element...  4.36 us
    slice x2, local copies, waits for them, and re-layouts, with_halo(): lax.slice_in_dim(block, block.shape[dim] - width, None, axis=dim)  3.34 us
    ppermute x8, waiting for transfers between devices, passed_along(): return lax.ppermute(array, axis, pairs)  3.25 us
  transfers between devices with their start and end apart: 15, of which 5 were waited for; matrix products, arithmetic and copies ran while one was open for 12% of the time, Pallas kernels for 0%

profile of v1, /device:TPU:0, one launch (start us, length us, event | category | flops | bytes accessed | tf_op | source)
XLA Modules:
  0.0 130.0 jit_solution(6738194803823368605)
XLA Ops:
  0.0 2.4 %fusion.30 = (bf16[1,48,48,128]{3,2,1,0:T(8,128)(2,1)}, bf16[1,48,48,128]{3,2,1,0:T(8,128)(2,1)}) fusion(bf16[2,48,48,128]{3,2,1,0:T(8,128)(2,1)} %param.7), kind=kLoop, calls=%fused_computation.63 | loop fusion | bytes 2359296 | tf_op jit(solution)/shard_map/slice | solution.py:50
  2.5 5.7 %collective-permute-start = (bf16[1,48,48,128]{3,2,1,0:T(8,128)(2,1)}, bf16[1,48,48,128]{3,2,1,0:T(8,128)(2,1)}, u32[]{:S(2)}, u32[]{:S(2)}) collective-permute-start(bf16[1,48,48,128]{3,2,1,0:T(8,128)(2,1)} %get-tuple-element.9), channel_id=1, source_target_pairs={{0,4},{4,8},{8,12},{12,16},{16,20},{20,24},{24,28},{1,5},{5,9},{9,... | collective-permute-start | bytes 1769480 | tf_op jit(solution)/shard_map/ppermute | solution.py:49
  10.1 4.5 %collective-permute-start.2 = (f32[8,128]{1,0:T(8,128)S(1)}, f32[8,128]{1,0:T(8,128)S(1)}, u32[]{:S(2)}, u32[]{:S(2)}) collective-permute-start(f32[8,128]{1,0:T(8,128)S(1)} %convolution_bitcast_fusion), channel_id=1, source_target_pairs={{0,4},{4,8},{8,12},{12,16},{16,20},{20,24},{24,28},{1,5},{5,9},{9,... | collective-permute-start | bytes 12296 | tf_op jit(solution)/shard_map/ppermute | solution.py:41
  14.7 1.3 collective-permute-start.3
  16.0 6.2 %collective-permute-start.4 = (f32[8,128]{1,0:T(8,128)S(1)}, f32[8,128]{1,0:T(8,128)}, u32[]{:S(2)}, u32[]{:S(2)}) collective-permute-start(f32[8,128]{1,0:T(8,128)S(1)} %convolution_bitcast_fusion), channel_id=1, source_target_pairs={{0,8},{4,12},{8,16},{12,20},{16,24},{20,28},{1,9},{5,13},{9,17},{1... | collective-permute-start | bytes 12296 | tf_op jit(solution)/shard_map/ppermute | solution.py:41
  22.4 1.8 %reshape.42 = bf16[8,4608]{1,0:T(8,128)(2,1)} reshape(bf16[8,2,48,48]{3,2,1,0:T(8,128)(2,1)} %param.9) | data formatting | bytes 147456 | tf_op jit(solution)/shard_map/reshape | solution.py:90
  24.2 1.5 %mul.62 = f32[4608]{0:T(1024)} reshape(f32[2,48,48]{2,1,0:T(8,128)} %param.8) | data formatting | bytes 36864 | tf_op jit(solution)/shard_map/mul | solution.py:80
  25.7 7.3 %collective-permute-done = bf16[1,48,48,128]{3,2,1,0:T(8,128)(2,1)} collective-permute-done((bf16[1,48,48,128]{3,2,1,0:T(8,128)(2,1)}, bf16[1,48,48,128]{3,2,1,0:T(8,128)(2,1)}, u32[]{:S(2)}, u32[]{:S(2)}) %collective-permute-start) | collective-permute-done | bytes 589856 | tf_op jit(solution)/shard_map/ppermute | solution.py:49
  34.3 1.6 %maximum_convert_fusion = f32[4,48,48,128]{3,2,1,0:T(8,128)S(1)} fusion(bf16[1,48,48,128]{3,2,1,0:T(8,128)(2,1)} %collective-permute-done.1, bf16[2,48,48,128]{3,2,1,0:T(8,128)(2,1)S(1)} %copy-done, bf16[1,48,48,128]{3,2,1,0:T(8,128)(2,1)} %collective-permute-done), kind=kLoop, calls=%fused_computation.34 | loop fusion | flops 3538944 | bytes 7077888 | tf_op jit(solution)/shard_map/convert_element_type | solution.py:68
  37.0 2.0 %fusion.19 = (f32[4608,128]{1,0:T(8,128)S(1)}, f32[4608,128]{1,0:T(8,128)S(1)}) fusion(f32[2,48,48,128]{3,2,1,0:T(8,128)S(1)} %fusion.12, f32[4608]{0:T(1024)S(1)} %copy-done.5, bf16[2,48,48,128]{3,2,1,0:T(8,128)(2,1)S(1)} %copy-done), kind=kLoop, calls=%fused_computation.38 | loop fusion | flops 2359296 | bytes 8275968 | tf_op jit(solution)/shard_map/add | solution.py:80
  39.0 1.4 %fusion.4 = bf16[4608,128]{1,0:T(8,128)(2,1)S(1)} fusion(f32[4608,128]{1,0:T(8,128)S(1)} %get-tuple-element.8, f32[4608,128]{1,0:T(8,128)S(1)} %get-tuple-element.7, f32[8,128]{1,0:T(8,128)S(1)} %collective-permute-done.5, f32[8,128]{1,0:T(8,128)} %collective-permute-done.4, f32[8,128]{1,0:T(8,128)S(1)} %collective-permute-done.3, ...), kind=kOutput, calls=%fused_computation.6 | convolution fusion | flops 11839488 | bytes 5992488 | tf_op jit(solution)/shard_map/dot_general | solution.py:76
  41.3 4.4 %collective-permute-start.6 = (bf16[1,48,48,128]{3,2,1,0:T(8,128)(2,1)}, bf16[1,48,48,128]{3,2,1,0:T(8,128)(2,1)S(1)}, u32[]{:S(2)}, u32[]{:S(2)}) collective-permute-start(bf16[1,48,48,128]{3,2,1,0:T(8,128)(2,1)} %bitcast.5), channel_id=1, source_target_pairs={{0,4},{4,8},{8,12},{12,16},{16,20},{20,24},{24,28},{1,5},{5,9},{9,... | collective-permute-start | bytes 1769480 | tf_op jit(solution)/shard_map/ppermute | solution.py:49
  45.8 1.3 collective-permute-start.7
  47.4 5.6 %collective-permute-start.10 = (f32[8,128]{1,0:T(8,128)S(1)}, f32[8,128]{1,0:T(8,128)S(1)}, u32[]{:S(2)}, u32[]{:S(2)}) collective-permute-start(f32[8,128]{1,0:T(8,128)S(1)} %fusion.28), channel_id=1, source_target_pairs={{0,8},{4,12},{8,16},{12,20},{16,24},{20,28},{1,9},{5,13},{9,17},{1... | collective-permute-start | bytes 12296 | tf_op jit(solution)/shard_map/ppermute | solution.py:41
  53.0 1.3 collective-permute-start.11
  54.3 3.5 %collective-permute-start.8 = (f32[8,128]{1,0:T(8,128)S(1)}, f32[8,128]{1,0:T(8,128)S(1)}, u32[]{:S(2)}, u32[]{:S(2)}) collective-permute-start(f32[8,128]{1,0:T(8,128)S(1)} %fusion.28), channel_id=1, source_target_pairs={{0,4},{4,8},{8,12},{12,16},{16,20},{20,24},{24,28},{1,5},{5,9},{9,... | collective-permute-start | bytes 12296 | tf_op jit(solution)/shard_map/ppermute | solution.py:41
  57.9 12.4 %collective-permute-done.6 = bf16[1,48,48,128]{3,2,1,0:T(8,128)(2,1)S(1)} collective-permute-done((bf16[1,48,48,128]{3,2,1,0:T(8,128)(2,1)}, bf16[1,48,48,128]{3,2,1,0:T(8,128)(2,1)S(1)}, u32[]{:S(2)}, u32[]{:S(2)}) %collective-permute-start.6) | collective-permute-done | bytes 589856 | tf_op jit(solution)/shard_map/ppermute | solution.py:49
  73.0 3.2 %collective-permute-done.9 = f32[8,128]{1,0:T(8,128)S(1)} collective-permute-done((f32[8,128]{1,0:T(8,128)S(1)}, f32[8,128]{1,0:T(8,128)S(1)}, u32[]{:S(2)}, u32[]{:S(2)}) %collective-permute-start.9) | collective-permute-done | bytes 4128 | tf_op jit(solution)/shard_map/ppermute | solution.py:41
  77.0 2.9 %constant_dynamic-update-slice_fusion.3 = (bf16[4608,512]{1,0:T(8,128)(2,1)S(1)}, bf16[4608,128]{1,0:T(8,128)(2,1)S(1)}) fusion(bf16[4608,512]{1,0:T(8,128)(2,1)S(1)} %broadcast_in_dim.22, s32[]{:T(128)S(6)} %select_n.36, f32[8,128]{1,0:T(8,128)S(1)} %collective-permute-done.11, f32[8,128]{1,0:T(8,128)S(1)} %collective-permute-done.10, ...), kind=kOutput, calls=%fused_computation.57 | convolution fusion | flops 14198784 | bytes 6013956 | tf_op jit(solution)/shard_map/dot_general | solution.py:76
  79.9 2.1 %copy-done.1 = bf16[4608,512]{1,0:T(8,128)(2,1)} copy-done((bf16[4608,512]{1,0:T(8,128)(2,1)}, bf16[4608,512]{1,0:T(8,128)(2,1)S(1)}, u32[]{:S(2)}) %copy-start.1) | copy-done | bytes 4718616
  82.1 1.7 %collective-permute-start.13 = (bf16[4608,128]{1,0:T(8,128)(2,1)S(1)}, bf16[4608,128]{1,0:T(8,128)(2,1)S(1)}, u32[]{:S(2)}, u32[]{:S(2)}) collective-permute-start(bf16[4608,128]{1,0:T(8,128)(2,1)S(1)} %get-tuple-element.12), channel_id=1, source_target_pairs={{0,3},{1,0},{2,1},{3,2},{4,7},{5,4},{6,5},{7,6},{8,11},{9,8},{10,9... | collective-permute-start | bytes 3538952 | tf_op jit(solution)/shard_map/ppermute | solution.py:26
  86.0 22.5 %collective-permute-done.12 = bf16[4608,128]{1,0:T(8,128)(2,1)S(1)} collective-permute-done((bf16[4608,128]{1,0:T(8,128)(2,1)S(1)}, bf16[4608,128]{1,0:T(8,128)(2,1)S(1)}, u32[]{:S(2)}, u32[]{:S(2)}) %collective-permute-start.12) | collective-permute-done | bytes 1179680 | tf_op jit(solution)/shard_map/ppermute | solution.py:19
  111.1 13.0 %collective-permute-done.14 = bf16[4608,128]{1,0:T(8,128)(2,1)S(1)} collective-permute-done((bf16[4608,128]{1,0:T(8,128)(2,1)S(1)}, bf16[4608,128]{1,0:T(8,128)(2,1)S(1)}, u32[]{:S(2)}, u32[]{:S(2)}) %collective-permute-start.14) | collective-permute-done | bytes 1179680 | tf_op jit(solution)/shard_map/ppermute | solution.py:19
  125.3 4.7 %convolution_convert_fusion = bf16[4608,128]{1,0:T(8,128)(2,1)} fusion(bf16[4608,512]{1,0:T(8,128)(2,1)} %constant_dynamic-update-slice_fusion, bf16[512,128]{1,0:T(8,128)(2,1)S(1)} %bitcast.34), kind=kOutput, calls=%fused_computation.8 | convolution fusion | flops 604569600 | bytes 6029312 | tf_op jit(solution)/shard_map/dot_general | solution.py:105
  (55 shorter events, 15.1 us)
Async XLA Ops:
  0.0 9.5 %copy-start = (bf16[2,48,48,128]{3,2,1,0:T(8,128)(2,1)S(1)}, bf16[2,48,48,128]{3,2,1,0:T(8,128)(2,1)}, u32[]{:S(2)}) copy-start(bf16[2,48,48,128]{3,2,1,0:T(8,128)(2,1)} %param.7) | copy-start | bytes 3538948
  0.0 9.4 %copy-start.10 = (s32[8]{0:T(128)S(1)}, s32[8]{0:T(128)}, u32[]{:S(2)}) copy-start(s32[8]{0:T(128)} %param.11) | copy-start | bytes 100
  0.0 9.4 %copy-start.3 = (bf16[8,2,48,48]{3,2,1,0:T(8,128)(2,1)S(1)}, bf16[8,2,48,48]{3,2,1,0:T(8,128)(2,1)}, u32[]{:S(2)}) copy-start(bf16[8,2,48,48]{3,2,1,0:T(8,128)(2,1)} %param.9) | copy-start | bytes 221188
  2.5 30.5 %collective-permute-start = (bf16[1,48,48,128]{3,2,1,0:T(8,128)(2,1)}, bf16[1,48,48,128]{3,2,1,0:T(8,128)(2,1)}, u32[]{:S(2)}, u32[]{:S(2)}) collective-permute-start(bf16[1,48,48,128]{3,2,1,0:T(8,128)(2,1)} %get-tuple-element.9), channel_id=1, source_target_pairs={{0,4},{4,8},{8,12},{12,16},{16,20},{20,24},{24,28},{1,5},{5,9},{9,... | collective-permute-start | bytes 1769480 | tf_op jit(solution)/shard_map/ppermute | solution.py:49
  8.1 26.1 %collective-permute-start.1 = (bf16[1,48,48,128]{3,2,1,0:T(8,128)(2,1)}, bf16[1,48,48,128]{3,2,1,0:T(8,128)(2,1)}, u32[]{:S(2)}, u32[]{:S(2)}) collective-permute-start(bf16[1,48,48,128]{3,2,1,0:T(8,128)(2,1)} %get-tuple-element.10), channel_id=1, source_target_pairs={{4,0},{8,4},{12,8},{16,12},{20,16},{24,20},{28,24},{5,1},{9,5},{13... | collective-permute-start | bytes 1769480 | tf_op jit(solution)/shard_map/ppermute | solution.py:52
  10.1 28.9 %collective-permute-start.2 = (f32[8,128]{1,0:T(8,128)S(1)}, f32[8,128]{1,0:T(8,128)S(1)}, u32[]{:S(2)}, u32[]{:S(2)}) collective-permute-start(f32[8,128]{1,0:T(8,128)S(1)} %convolution_bitcast_fusion), channel_id=1, source_target_pairs={{0,4},{4,8},{8,12},{12,16},{16,20},{20,24},{24,28},{1,5},{5,9},{9,... | collective-permute-start | bytes 12296 | tf_op jit(solution)/shard_map/ppermute | solution.py:41
  14.7 24.3 %collective-permute-start.3 = (f32[8,128]{1,0:T(8,128)S(1)}, f32[8,128]{1,0:T(8,128)S(1)}, u32[]{:S(2)}, u32[]{:S(2)}) collective-permute-start(f32[8,128]{1,0:T(8,128)S(1)} %convolution_bitcast_fusion), channel_id=1, source_target_pairs={{4,0},{8,4},{12,8},{16,12},{20,16},{24,20},{28,24},{5,1},{9,5},{13... | collective-permute-start | bytes 12296 | tf_op jit(solution)/shard_map/ppermute | solution.py:41
  16.0 23.0 %collective-permute-start.4 = (f32[8,128]{1,0:T(8,128)S(1)}, f32[8,128]{1,0:T(8,128)}, u32[]{:S(2)}, u32[]{:S(2)}) collective-permute-start(f32[8,128]{1,0:T(8,128)S(1)} %convolution_bitcast_fusion), channel_id=1, source_target_pairs={{0,8},{4,12},{8,16},{12,20},{16,24},{20,28},{1,9},{5,13},{9,17},{1... | collective-permute-start | bytes 12296 | tf_op jit(solution)/shard_map/ppermute | solution.py:41
  33.0 6.0 %collective-permute-start.5 = (f32[8,128]{1,0:T(8,128)S(1)}, f32[8,128]{1,0:T(8,128)S(1)}, u32[]{:S(2)}, u32[]{:S(2)}) collective-permute-start(f32[8,128]{1,0:T(8,128)S(1)} %convolution_bitcast_fusion), channel_id=1, source_target_pairs={{8,0},{12,4},{16,8},{20,12},{24,16},{28,20},{9,1},{13,5},{17,9},{2... | collective-permute-start | bytes 12296 | tf_op jit(solution)/shard_map/ppermute | solution.py:41
  35.9 1.1 copy-start.5
  36.9 2.1 %copy-start.2 = (bf16[8,4608]{1,0:T(8,128)(2,1)S(1)}, bf16[8,4608]{1,0:T(8,128)(2,1)}, u32[]{:S(2)}) copy-start(bf16[8,4608]{1,0:T(8,128)(2,1)} %reshape.42) | copy-start | bytes 221188
  36.9 2.1 %copy-start.7 = (f32[8]{0:T(128)S(1)}, f32[8]{0:T(128)}, u32[]{:S(2)}) copy-start(f32[8]{0:T(128)} %param.10) | copy-start | bytes 100
  41.3 29.0 %collective-permute-start.6 = (bf16[1,48,48,128]{3,2,1,0:T(8,128)(2,1)}, bf16[1,48,48,128]{3,2,1,0:T(8,128)(2,1)S(1)}, u32[]{:S(2)}, u32[]{:S(2)}) collective-permute-start(bf16[1,48,48,128]{3,2,1,0:T(8,128)(2,1)} %bitcast.5), channel_id=1, source_target_pairs={{0,4},{4,8},{8,12},{12,16},{16,20},{20,24},{24,28},{1,5},{5,9},{9,... | collective-permute-start | bytes 1769480 | tf_op jit(solution)/shard_map/ppermute | solution.py:49
  45.8 25.9 %collective-permute-start.7 = (bf16[1,48,48,128]{3,2,1,0:T(8,128)(2,1)S(1)}, bf16[1,48,48,128]{3,2,1,0:T(8,128)(2,1)S(1)}, u32[]{:S(2)}, u32[]{:S(2)}) collective-permute-start(bf16[1,48,48,128]{3,2,1,0:T(8,128)(2,1)S(1)} %bitcast.33), channel_id=1, source_target_pairs={{4,0},{8,4},{12,8},{16,12},{20,16},{24,20},{28,24},{5,1},{9,5},{13... | collective-permute-start | bytes 1769480 | tf_op jit(solution)/shard_map/ppermute | solution.py:52
  47.4 25.6 %collective-permute-start.10 = (f32[8,128]{1,0:T(8,128)S(1)}, f32[8,128]{1,0:T(8,128)S(1)}, u32[]{:S(2)}, u32[]{:S(2)}) collective-permute-start(f32[8,128]{1,0:T(8,128)S(1)} %fusion.28), channel_id=1, source_target_pairs={{0,8},{4,12},{8,16},{12,20},{16,24},{20,28},{1,9},{5,13},{9,17},{1... | collective-permute-start | bytes 12296 | tf_op jit(solution)/shard_map/ppermute | solution.py:41
  53.0 20.0 %collective-permute-start.11 = (f32[8,128]{1,0:T(8,128)S(1)}, f32[8,128]{1,0:T(8,128)S(1)}, u32[]{:S(2)}, u32[]{:S(2)}) collective-permute-start(f32[8,128]{1,0:T(8,128)S(1)} %fusion.28), channel_id=1, source_target_pairs={{8,0},{12,4},{16,8},{20,12},{24,16},{28,20},{9,1},{13,5},{17,9},{2... | collective-permute-start | bytes 12296 | tf_op jit(solution)/shard_map/ppermute | solution.py:41
  54.3 18.7 %collective-permute-start.8 = (f32[8,128]{1,0:T(8,128)S(1)}, f32[8,128]{1,0:T(8,128)S(1)}, u32[]{:S(2)}, u32[]{:S(2)}) collective-permute-start(f32[8,128]{1,0:T(8,128)S(1)} %fusion.28), channel_id=1, source_target_pairs={{0,4},{4,8},{8,12},{12,16},{16,20},{20,24},{24,28},{1,5},{5,9},{9,... | collective-permute-start | bytes 12296 | tf_op jit(solution)/shard_map/ppermute | solution.py:41
  70.4 5.9 %collective-permute-start.9 = (f32[8,128]{1,0:T(8,128)S(1)}, f32[8,128]{1,0:T(8,128)S(1)}, u32[]{:S(2)}, u32[]{:S(2)}) collective-permute-start(f32[8,128]{1,0:T(8,128)S(1)} %fusion.28), channel_id=1, source_target_pairs={{4,0},{8,4},{12,8},{16,12},{20,16},{24,20},{28,24},{5,1},{9,5},{13... | collective-permute-start | bytes 12296 | tf_op jit(solution)/shard_map/ppermute | solution.py:41
  77.0 5.1 %copy-start.9 = (s32[12,2]{0,1:T(2,128)S(1)}, s32[12,2]{0,1:T(2,128)}, u32[]{:S(2)}) copy-start(s32[12,2]{0,1:T(2,128)} %param.12) | copy-start | bytes 292
  79.9 2.1 %copy-start.1 = (bf16[4608,512]{1,0:T(8,128)(2,1)}, bf16[4608,512]{1,0:T(8,128)(2,1)S(1)}, u32[]{:S(2)}) copy-start(bf16[4608,512]{1,0:T(8,128)(2,1)S(1)} %get-tuple-element.11) | copy-start | bytes 14155780
  82.1 26.4 %collective-permute-start.12 = (bf16[4608,128]{1,0:T(8,128)(2,1)S(1)}, bf16[4608,128]{1,0:T(8,128)(2,1)S(1)}, u32[]{:S(2)}, u32[]{:S(2)}) collective-permute-start(bf16[4608,128]{1,0:T(8,128)(2,1)S(1)} %get-tuple-element.12), channel_id=1, source_target_pairs={{0,1},{1,2},{2,3},{3,0},{4,5},{5,6},{6,7},{7,4},{8,9},{9,10},{10,1... | collective-permute-start | bytes 3538952 | tf_op jit(solution)/shard_map/ppermute | solution.py:19
  82.1 27.8 %collective-permute-start.13 = (bf16[4608,128]{1,0:T(8,128)(2,1)S(1)}, bf16[4608,128]{1,0:T(8,128)(2,1)S(1)}, u32[]{:S(2)}, u32[]{:S(2)}) collective-permute-start(bf16[4608,128]{1,0:T(8,128)(2,1)S(1)} %get-tuple-element.12), channel_id=1, source_target_pairs={{0,3},{1,0},{2,1},{3,2},{4,7},{5,4},{6,5},{7,6},{8,11},{9,8},{10,9... | collective-permute-start | bytes 3538952 | tf_op jit(solution)/shard_map/ppermute | solution.py:26
  108.4 15.6 %collective-permute-start.14 = (bf16[4608,128]{1,0:T(8,128)(2,1)S(1)}, bf16[4608,128]{1,0:T(8,128)(2,1)S(1)}, u32[]{:S(2)}, u32[]{:S(2)}) collective-permute-start(bf16[4608,128]{1,0:T(8,128)(2,1)S(1)} %collective-permute-done.12), channel_id=1, source_target_pairs={{0,1},{1,2},{2,3},{3,0},{4,5},{5,6},{6,7},{7,4},{8,9},{9,10},{10,1... | collective-permute-start | bytes 3538952 | tf_op jit(solution)/shard_map/ppermute | solution.py:19
  109.8 15.4 %copy-start.4 = (bf16[4,128,128]{2,1,0:T(8,128)(2,1)S(1)}, bf16[4,128,128]{2,1,0:T(8,128)(2,1)}, u32[]{:S(2)}) copy-start(bf16[4,128,128]{2,1,0:T(8,128)(2,1)} %copy.12) | copy-start | bytes 393220
  (2 other events, 1.5 us)
